TPU v7x, 128 devices: a whole 4x4x4 slice. The times are simulated.
128 devices in a mesh: bricks: 128 (over y, z, x, core).
Axes of the slice: x: 4, y: 4, z: 4, core: 2. Of those that a mesh axis runs over, the one named last changes fastest.
Arguments:
- calcium: float32 [256, 32, 1024], P('bricks'), may hold values from 0.2 to 1.5
- buffer: float32 [256, 32, 1024], P('bricks'), may hold values from 0.1 to 1.5
- fraction: float32 [256, 32, 1024], P('bricks'), may hold values from 0.1 to 0.4
- rates: float32 [256, 3, 2], P('bricks'), may hold values from 2 to 64
- inverses: float32 [256, 3, 2, 32, 32], P('bricks'), as said below
- neighbors: int32 [3, 2, 256], replicated, may hold values from -1 to 255, as said below
- ranks: int32 [3, 256], replicated, may hold values from 0 to 31, as said below
Outputs:
- calcium_next: float32 [256, 32, 1024], P('bricks')
- buffer_next: float32 [256, 32, 1024], P('bricks')
Inputs may be any that keep to these rules, and one draw needn't show every extreme that they name: neighbors[d, 0, s] and neighbors[d, 1, s] are the slots of the active bricks adjacent to slot s before and after it along dimension d of a block of 32 x 16 x 2 brick positions, -1 where that position is inactive or outside; active bricks fill whole rows along the first dimension. ranks[d, s] is the number of consecutive active bricks before slot s along dimension d. inverses[s, d, k] is the inverse of I + rates[s, d, k] K, K the 32 x 32 second difference with diagonal 1, 2, ..., 2, 1 and off-diagonals -1.
All inputs are finite; a program needn't handle non-finite values.
Results may differ from a plain program's by a relative error of at most 0.00015.
Values sent between devices are 32-bit elements; how exact they have to be, the bound alone decides.
A program may use at most 128 MiB of HBM per device.

v0:
```python
from functools import partial
import jax
import jax.numpy as jnp
from jax import lax
from jax.sharding import PartitionSpec as P

GX = 32
KON = 0.5
KOFF = 0.3
BTOT = 2.0
INFLUX = 0.1


def fetch(table, index):
    rows = jnp.take(table, jnp.maximum(index, 0), axis=0)
    has = (index >= 0).reshape((-1,) + (1,) * (rows.ndim - 1))
    return jnp.where(has, rows, jnp.zeros_like(rows))


def lookup(planes, before, after):
    sides = []
    for d in range(3):
        lower = fetch(planes[:, d, 1], before[d])
        upper = fetch(planes[:, d, 0], after[d])
        sides.append(jnp.stack([lower, upper], 1))
    return jnp.stack(sides, 1)


def coupling(rate_all, neighbors):
    per_dim = []
    for d in range(3):
        mine = rate_all[:, d]
        sides = []
        for side in range(2):
            other = fetch(mine, neighbors[d, side])
            has = (neighbors[d, side] >= 0)[:, None]
            sides.append(jnp.where(has, 2.0 * mine * other / (mine + other), jnp.zeros_like(mine)))
        per_dim.append(jnp.stack(sides, 1))
    return jnp.stack(per_dim, 1)


def end_planes(field):
    count, edge = (field.shape[0], field.shape[2])
    per_dim = []
    for d in range(3):
        first = lax.index_in_dim(field, 0, 2 + d, False).reshape(count, 2, edge * edge)
        last = lax.index_in_dim(field, edge - 1, 2 + d, False).reshape(count, 2, edge * edge)
        per_dim.append(jnp.stack([first, last], 1))
    return jnp.stack(per_dim, 1)


def operator(field, d, rate, glow, gup, hlow, hup):
    axis = 2 + d
    edge = field.shape[axis]
    plane_shape = lax.index_in_dim(field, 0, axis, False).shape
    lower_face = jnp.expand_dims(hlow.reshape(plane_shape), axis)
    upper_face = jnp.expand_dims(hup.reshape(plane_shape), axis)
    upper = jnp.concatenate([lax.slice_in_dim(field, 1, edge, axis=axis), upper_face], axis)
    lower = jnp.concatenate([lower_face, lax.slice_in_dim(field, 0, edge - 1, axis=axis)], axis)
    place = lax.broadcasted_iota(jnp.int32, field.shape, axis)
    inner = rate[:, :, None, None, None]
    c_up = jnp.where(place == edge - 1, gup[:, :, None, None, None], inner)
    c_down = jnp.where(place == 0, glow[:, :, None, None, None], inner)
    return c_up * (upper - field) + c_down * (lower - field)


def reaction(field, fraction):
    count, edge = (field.shape[0], field.shape[2])
    alpha = fraction.reshape(count, edge, edge, edge)
    calc, bound = (field[:, 0], field[:, 1])
    bind = KON * calc * (BTOT - bound) - KOFF * bound
    return jnp.stack([-bind + INFLUX * (1.0 - alpha) / alpha, bind], 1)


def apply_inverse(block, field, d):
    forms = ["psab,psbjk->psajk", "psab,psibk->psiak", "psab,psijb->psija"]
    return jnp.einsum(forms[d], block, field, precision=lax.Precision.HIGHEST)


def line_ends(field, d):
    count, edge = (field.shape[0], field.shape[2])
    first = lax.index_in_dim(field, 0, 2 + d, False).reshape(count, 2, edge * edge)
    last = lax.index_in_dim(field, edge - 1, 2 + d, False).reshape(count, 2, edge * edge)
    return jnp.stack([first, last], 2)


def block_terms(glow, gup, corner):
    v_first, v_last, w_first, w_last = (
        corner[..., 0],
        corner[..., 1],
        corner[..., 2],
        corner[..., 3],
    )
    a00 = 1.0 + glow * v_first
    a01 = gup * w_first
    a10 = glow * v_last
    a11 = 1.0 + gup * w_last
    lq0 = -glow * v_first
    lq1 = -glow * v_last
    up0 = -gup * w_first
    up1 = -gup * w_last
    return (a00, a01, a10, a11, lq0, lq1, up0, up1)


def chain_order(before, rank):
    slots = jnp.arange(before.shape[0], dtype=jnp.int32)
    pointer = jnp.where(before >= 0, before, slots)
    for step in range(GX.bit_length()):
        pointer = jnp.take(pointer, pointer, axis=0)
    sort_key = pointer * GX + rank
    order = jnp.argsort(sort_key)
    inverse_order = jnp.argsort(order)
    return (order, inverse_order)


def shift_down(values):
    return jnp.concatenate([jnp.zeros_like(values[:1]), values[:-1]], 0)


def shift_up(values):
    return jnp.concatenate([values[1:], jnp.zeros_like(values[:1])], 0)


def compose_maps(first_map, second_map):
    e00, e01, e10, e11 = first_map
    l00, l01, l10, l11 = second_map
    n00 = l00 * e00 + l01 * e10
    n01 = l00 * e01 + l01 * e11
    n10 = l10 * e00 + l11 * e10
    n11 = l10 * e01 + l11 * e11
    scale = jnp.abs(n00) + jnp.abs(n01) + jnp.abs(n10) + jnp.abs(n11)
    return (n00 / scale, n01 / scale, n10 / scale, n11 / scale)


def compose_affine(first_map, second_map):
    first_q, first_p = first_map
    second_q, second_p = second_map
    return (first_q * second_q, second_p + second_q * first_p)


def sorted_solve(glow, gup, corner, before, after, order, inverse_order, ends):
    glow = jnp.take(glow, order, axis=0)
    gup = jnp.take(gup, order, axis=0)
    corner = jnp.take(corner, order, axis=0)
    has_b = jnp.take(before, order, axis=0) >= 0
    has_a = jnp.take(after, order, axis=0) >= 0
    arranged = jnp.take(ends, order, axis=0)
    y0 = arranged[:, :, 0]
    y1 = arranged[:, :, 1]
    a00, a01, a10, a11, lq0, lq1, up0, up1 = block_terms(glow, gup, corner)
    maps = (
        -(lq0 * up1 - lq1 * up0),
        a00 * up1 - a10 * up0,
        -(lq0 * a11 - a01 * lq1),
        a00 * a11 - a01 * a10,
    )
    summed = lax.associative_scan(compose_maps, maps, axis=0)
    f1_prev = summed[1] / summed[3]
    fq = shift_down(f1_prev)
    b00 = a00 - lq0 * fq
    b10 = a10 - lq1 * fq
    det = b00 * a11 - a01 * b10
    f0 = (a11 * up0 - a01 * up1) / det
    f1 = (b00 * up1 - b10 * up0) / det
    slope = (-(b00 * lq1 - b10 * lq0) / det)[:, :, None]
    offset = (b00[:, :, None] * y1 - b10[:, :, None] * y0) / det[:, :, None]
    e1 = lax.associative_scan(compose_affine, (slope, offset), axis=0)[1]
    eq = shift_down(e1)
    e0 = (
        a11[:, :, None] * y0 - a01[:, :, None] * y1 - (a11 * lq0 - a01 * lq1)[:, :, None] * eq
    ) / det[:, :, None]
    zp = lax.associative_scan(compose_affine, (-f0[:, :, None], e0), reverse=True, axis=0)[1]
    pn = shift_up(zp)
    zq = e1 - f1[:, :, None] * pn
    low = jnp.where(has_b[:, None, None], zp - shift_down(zq), jnp.zeros_like(zp))
    high = jnp.where(has_a[:, None, None], zq - pn, jnp.zeros_like(zq))
    return jnp.take(jnp.stack([low, high], 2), inverse_order, axis=0)


def correct(local, block, glow, gup, jumps, d):
    axis = 2 + d
    count, edge = (local.shape[0], local.shape[2])
    shape_v = [count, 2, 1, 1, 1]
    shape_v[axis] = edge
    first_col = block[..., 0].reshape(shape_v)
    last_col = block[..., edge - 1].reshape(shape_v)
    plane_shape = lax.index_in_dim(local, 0, axis, False).shape
    low = jnp.expand_dims(jumps[:, :, 0].reshape(plane_shape), axis)
    high = jnp.expand_dims(jumps[:, :, 1].reshape(plane_shape), axis)
    return (
        local
        - glow[:, :, None, None, None] * low * first_col
        - gup[:, :, None, None, None] * high * last_col
    )


def body(calcium, buffer, fraction, rates, inverses, neighbors, ranks):
    count, edge = (calcium.shape[0], calcium.shape[1])
    devices = lax.axis_size("bricks")
    square = edge * edge
    per_device = square // devices
    start = lax.axis_index("bricks") * count
    corners = jnp.stack(
        [
            inverses[..., 0, 0],
            inverses[..., edge - 1, 0],
            inverses[..., 0, edge - 1],
            inverses[..., edge - 1, edge - 1],
        ],
        -1,
    )
    rate_all, corner_all = (
        lax.all_gather(rates, "bricks", axis=0, tiled=True),
        lax.all_gather(corners, "bricks", axis=0, tiled=True),
    )
    couple_all = coupling(rate_all, neighbors)
    couple = lax.dynamic_slice_in_dim(couple_all, start, count, 0)
    field = jnp.stack([calcium, buffer], 1).reshape(count, 2, edge, edge, edge)
    planes = end_planes(field).reshape(count, 3, 2, 2, devices, per_device)
    lined = lookup(
        lax.all_to_all(planes, "bricks", split_axis=4, concat_axis=0, tiled=True),
        neighbors[:, 0],
        neighbors[:, 1],
    )
    halos = lax.all_to_all(lined, "bricks", split_axis=0, concat_axis=4, tiled=True).reshape(
        count, 3, 2, 2, square
    )
    lams = [
        operator(
            field, d, rates[:, d], couple[:, d, 0], couple[:, d, 1], halos[:, d, 0], halos[:, d, 1]
        )
        for d in range(3)
    ]
    rhs = field + lams[0] + 2.0 * lams[1] + 2.0 * lams[2] + reaction(field, fraction)

    def solve(right, d):
        block = inverses[:, d]
        local = apply_inverse(block, right, d)
        ends = line_ends(local, d).reshape(count, 2, 2, devices, per_device)
        order, inverse_order = chain_order(neighbors[d, 0], ranks[d])
        chain_fn = partial(
            sorted_solve,
            couple_all[:, d, 0],
            couple_all[:, d, 1],
            corner_all[:, d],
            neighbors[d, 0],
            neighbors[d, 1],
            order,
            inverse_order,
        )
        lined_jumps = chain_fn(
            lax.all_to_all(ends, "bricks", split_axis=3, concat_axis=0, tiled=True)[:, :, :, 0]
        )[:, :, :, None]
        jumps = lax.all_to_all(
            lined_jumps, "bricks", split_axis=0, concat_axis=3, tiled=True
        ).reshape(count, 2, 2, square)
        return correct(local, block, couple[:, d, 0], couple[:, d, 1], jumps, d)

    first = solve(rhs, 0)
    second = solve(first - lams[1], 1)
    third = solve(second - lams[2], 2)
    result = third.reshape(count, 2, edge, edge * edge)
    return (result[:, 0], result[:, 1])


def solution(mesh):
    in_specs = (
        P("bricks", None, None),
        P("bricks", None, None),
        P("bricks", None, None),
        P("bricks", None, None),
        P("bricks", None, None, None, None),
        P(),
        P(),
    )
    out_specs = (P("bricks", None, None), P("bricks", None, None))
    return jax.shard_map(body, mesh=mesh, in_specs=in_specs, out_specs=out_specs, check_vma=False)
```

profile of v0, /device:TPU:1, one launch (start us, length us, event | category | flops | bytes accessed | tf_op | source)
XLA Modules:
  0.0 658.5 jit_solution(8018914261589705422)
XLA Ops:
  5.6 5.8 divide_add_fusion
  23.9 4.2 reshape.1049
  28.1 12.3 %all-to-all-start = ((f32[128,1,192]{2,1,0:T(1,128)}), f32[128,1,192]{2,1,0:T(1,128)}, u32[]{:S(2)}, u32[]{:S(2)}) async-start(f32[128,1,192]{2,1,0:T(1,128)} %reshape.1049), calls=%async_computation | async-start | bytes 262144 | tf_op jit(solution)/shard_map/all_to_all | solution.py:221
  53.0 3.2 sort.91
  56.2 3.2 sort.92
  63.8 38.2 %all_gather.7 = f32[256,3,2,4]{1,2,0,3:T(2,128)S(1)} all-gather(f32[2,3,2,4]{1,2,0,3:T(2,128)S(1)} %pad_maximum_fusion.7), channel_id=1, replica_groups=mesh['bricks'=128] {'bricks'}, dimensions={0}, use_global_device_ids=true | all-gather | bytes 24768 | tf_op jit(solution)/shard_map/all_gather | solution.py:214
  102.1 3.6 fusion.208
  114.2 33.5 %all_gather.6 = f32[256,3,2]{1,2,0:T(2,128)S(1)} all-gather(f32[2,3,2]{1,2,0:T(2,128)S(1)} %copy-done.20), channel_id=1, replica_groups=mesh['bricks'=128] {'bricks'}, dimensions={0}, use_global_device_ids=true | all-gather | bytes 6192 | tf_op jit(solution)/shard_map/all_gather | solution.py:213
  197.8 3.2 sort.89
  201.0 3.2 sort.90
  260.9 3.2 sort.87
  264.1 3.2 sort.88
  307.0 3.2 fusion.204
  338.7 3.2 reshape.1050
  374.5 4.2 reshape.1051
  378.8 5.8 all-to-all-start.1
  384.6 9.9 %all-to-all-done.1 = f32[128,1,192]{2,1,0:T(1,128)S(1)} async-done(((f32[128,1,192]{2,1,0:T(1,128)}), f32[128,1,192]{2,1,0:T(1,128)S(1)}, u32[]{:S(2)}, u32[]{:S(2)}) %all-to-all-start.1) | async-done | bytes 98336 | tf_op jit(solution)/shard_map/all_to_all | solution.py:225
  410.5 4.8 fusion.18
  417.5 3.8 fusion.31
  424.3 4.2 all-to-all-start.2
  477.1 9.7 %all-to-all-start.3 = ((f32[256,2,2,1,8]{4,2,1,3,0:T(2,128)}), f32[256,2,2,1,8]{4,2,1,3,0:T(2,128)S(1)}, u32[]{:S(2)}, u32[]{:S(2)}) async-start(f32[256,2,2,1,8]{4,2,1,3,0:T(2,128)} %select_bitcast_fusion.2), calls=%async_computation.3 | async-start | bytes 1048576 | tf_op jit(solution)/shard_map/all_to_all | solution.py:254
  487.7 12.5 %all-to-all-done.3 = f32[256,2,2,1,8]{4,2,1,3,0:T(2,128)S(1)} async-done(((f32[256,2,2,1,8]{4,2,1,3,0:T(2,128)}), f32[256,2,2,1,8]{4,2,1,3,0:T(2,128)S(1)}, u32[]{:S(2)}, u32[]{:S(2)}) %all-to-all-start.3) | async-done | bytes 32800 | tf_op jit(solution)/shard_map/all_to_all | solution.py:254
  501.2 3.7 subtract_subtract_fusion.1
  504.9 3.2 fusion.25
  511.0 4.9 all-to-all-start.4
  556.6 9.6 %all-to-all-start.5 = ((f32[256,2,2,1,8]{4,1,2,3,0:T(2,128)}), f32[256,2,2,1,8]{4,1,2,3,0:T(2,128)S(1)}, u32[]{:S(2)}, u32[]{:S(2)}) async-start(f32[256,2,2,1,8]{4,1,2,3,0:T(2,128)} %copy.2505), calls=%async_computation.5 | async-start | bytes 1048576 | tf_op jit(solution)/shard_map/all_to_all | solution.py:254
  566.6 13.1 %all-to-all-done.5 = f32[256,2,2,1,8]{4,1,2,3,0:T(2,128)S(1)} async-done(((f32[256,2,2,1,8]{4,1,2,3,0:T(2,128)}), f32[256,2,2,1,8]{4,1,2,3,0:T(2,128)S(1)}, u32[]{:S(2)}, u32[]{:S(2)}) %all-to-all-start.5) | async-done | bytes 32800 | tf_op jit(solution)/shard_map/all_to_all | solution.py:254
  580.5 3.7 subtract_subtract_fusion
  584.3 9.1 %fusion.23 = f32[2,2,32,32,32]{3,4,2,1,0:T(8,128)S(1)} fusion(f32[2,2,32,32,32]{4,2,3,1,0:T(8,128)S(1)} %subtract_subtract_fusion, f32[2,3,2,32,32]{4,3,2,1,0:T(8,128)S(1)} %copy-done.18), kind=kOutput, calls=%fused_computation.78 | convolution fusion | flops 50331648 | bytes 2686976 | tf_op jit(solution)/shard_map/psab,psijb->psija/dot_general | solution.py:77
  595.3 4.9 all-to-all-start.6
  602.2 11.5 %all-to-all-done.6 = f32[2,2,2,128,8]{4,1,0,2,3:T(2,128)S(1)} async-done(((f32[2,2,2,128,8]{4,1,0,2,3:T(2,128)}), f32[2,2,2,128,8]{4,1,0,2,3:T(2,128)S(1)}, u32[]{:S(2)}, u32[]{:S(2)}) %all-to-all-start.6) | async-done | bytes 32800 | tf_op jit(solution)/shard_map/all_to_all | solution.py:252
  633.6 18.0 %all_to_all.123 = f32[256,2,2,1,8]{4,1,2,3,0:T(2,128)S(1)} all-to-all(f32[256,2,2,1,8]{4,1,2,3,0:T(2,128)S(1)} %copy.2524), channel_id=1, replica_groups=mesh['bricks'=128] {'bricks'}, dimensions={0} | all-to-all | bytes 65536 | tf_op jit(solution)/shard_map/all_to_all | solution.py:254
  (2114 shorter events, 390.8 us)
Async XLA Ops:
  28.1 308.1 %all-to-all-start = ((f32[128,1,192]{2,1,0:T(1,128)}), f32[128,1,192]{2,1,0:T(1,128)}, u32[]{:S(2)}, u32[]{:S(2)}) async-start(f32[128,1,192]{2,1,0:T(1,128)} %reshape.1049), calls=%async_computation | async-start | bytes 262144 | tf_op jit(solution)/shard_map/all_to_all | solution.py:221
  187.1 30.3 %copy-start.196 = (pred[256]{0:T(512)(128)(4,1)}, pred[256]{0:T(512)(128)(4,1)S(1)}, u32[]{:S(2)}) copy-start(pred[256]{0:T(512)(128)(4,1)S(1)} %get-tuple-element.622) | copy-start | bytes 772
  187.1 30.3 %copy-start.198 = (pred[256]{0:T(512)(128)(4,1)}, pred[256]{0:T(512)(128)(4,1)S(1)}, u32[]{:S(2)}) copy-start(pred[256]{0:T(512)(128)(4,1)S(1)} %get-tuple-element.623) | copy-start | bytes 772
  187.1 30.3 %copy-start.200 = (pred[256]{0:T(512)(128)(4,1)}, pred[256]{0:T(512)(128)(4,1)S(1)}, u32[]{:S(2)}) copy-start(pred[256]{0:T(512)(128)(4,1)S(1)} %get-tuple-element.646) | copy-start | bytes 772
  187.2 30.3 %copy-start.202 = (pred[256]{0:T(512)(128)(4,1)}, pred[256]{0:T(512)(128)(4,1)S(1)}, u32[]{:S(2)}) copy-start(pred[256]{0:T(512)(128)(4,1)S(1)} %get-tuple-element.647) | copy-start | bytes 772
  248.8 27.4 %copy-start.204 = (pred[256]{0:T(512)(128)(4,1)}, pred[256]{0:T(512)(128)(4,1)S(1)}, u32[]{:S(2)}) copy-start(pred[256]{0:T(512)(128)(4,1)S(1)} %get-tuple-element.618) | copy-start | bytes 772
  248.9 27.4 %copy-start.206 = (pred[256]{0:T(512)(128)(4,1)}, pred[256]{0:T(512)(128)(4,1)S(1)}, u32[]{:S(2)}) copy-start(pred[256]{0:T(512)(128)(4,1)S(1)} %get-tuple-element.619) | copy-start | bytes 772
  248.9 27.4 %copy-start.208 = (pred[256]{0:T(512)(128)(4,1)}, pred[256]{0:T(512)(128)(4,1)S(1)}, u32[]{:S(2)}) copy-start(pred[256]{0:T(512)(128)(4,1)S(1)} %get-tuple-element.648) | copy-start | bytes 772
  248.9 27.4 %copy-start.210 = (pred[256]{0:T(512)(128)(4,1)}, pred[256]{0:T(512)(128)(4,1)S(1)}, u32[]{:S(2)}) copy-start(pred[256]{0:T(512)(128)(4,1)S(1)} %get-tuple-element.649) | copy-start | bytes 772
  276.6 30.2 %copy-start.7 = (f32[256,1,2,2]{3,0,2,1:T(8,128)S(1)}, f32[256,1,2,2]{3,0,2,1:T(8,128)}, u32[]{:S(2)}) copy-start(f32[256,1,2,2]{3,0,2,1:T(8,128)} %copy-done.6) | copy-start | bytes 12292
  276.6 30.3 %copy-start.5 = (f32[256,1,2,2]{3,0,2,1:T(8,128)S(1)}, f32[256,1,2,2]{3,0,2,1:T(8,128)}, u32[]{:S(2)}) copy-start(f32[256,1,2,2]{3,0,2,1:T(8,128)} %copy-done.4) | copy-start | bytes 12292
  302.8 31.3 %copy-start.126 = (f32[2,2,1]{0,1,2:T(2,128)}, f32[2,2,1]{0,1,2:T(2,128)S(1)}, u32[]{:S(2)}) copy-start(f32[2,2,1]{0,1,2:T(2,128)S(1)} %slice.3220) | copy-start | bytes 52
  306.6 27.6 %copy-start.159 = (f32[2,2,1]{0,1,2:T(2,128)}, f32[2,2,1]{0,1,2:T(2,128)S(1)}, u32[]{:S(2)}) copy-start(f32[2,2,1]{0,1,2:T(2,128)S(1)} %slice.3154) | copy-start | bytes 52
  327.9 82.4 %copy-start.88 = (f32[2,1,1,2]{3,0,2,1:T(2,128)}, f32[2,1,1,2]{3,0,2,1:T(2,128)S(1)}, u32[]{:S(2)}) copy-start(f32[2,1,1,2]{3,0,2,1:T(2,128)S(1)} %copy.2457) | copy-start | bytes 52
  328.0 82.4 %copy-start.90 = (f32[2,1,1,2]{3,0,2,1:T(2,128)}, f32[2,1,1,2]{3,0,2,1:T(2,128)S(1)}, u32[]{:S(2)}) copy-start(f32[2,1,1,2]{3,0,2,1:T(2,128)S(1)} %copy.2459) | copy-start | bytes 52
  328.0 87.2 %copy-start.92 = (f32[2,1,1,2]{3,0,2,1:T(2,128)}, f32[2,1,1,2]{3,0,2,1:T(2,128)S(1)}, u32[]{:S(2)}) copy-start(f32[2,1,1,2]{3,0,2,1:T(2,128)S(1)} %copy.2455) | copy-start | bytes 52
  378.8 15.8 %all-to-all-start.1 = ((f32[128,1,192]{2,1,0:T(1,128)}), f32[128,1,192]{2,1,0:T(1,128)S(1)}, u32[]{:S(2)}, u32[]{:S(2)}) async-start(f32[128,1,192]{2,1,0:T(1,128)} %reshape.1051), calls=%async_computation.1 | async-start | bytes 262144 | tf_op jit(solution)/shard_map/all_to_all | solution.py:225
  384.6 30.7 %copy-start.244 = (pred[32]{0:T(512)(128)(4,1)}, pred[32]{0:T(512)(128)(4,1)S(1)}, u32[]{:S(2)}) copy-start(pred[32]{0:T(512)(128)(4,1)S(1)} %get-tuple-element.654) | copy-start | bytes 100
  384.6 30.7 %copy-start.246 = (pred[32]{0:T(512)(128)(4,1)}, pred[32]{0:T(512)(128)(4,1)S(1)}, u32[]{:S(2)}) copy-start(pred[32]{0:T(512)(128)(4,1)S(1)} %get-tuple-element.655) | copy-start | bytes 100
  424.3 17.9 %all-to-all-start.2 = ((f32[2,2,2,128,8]{4,1,0,2,3:T(2,128)}), f32[2,2,2,128,8]{4,1,0,2,3:T(2,128)S(1)}, u32[]{:S(2)}, u32[]{:S(2)}) async-start(f32[2,2,2,128,8]{4,1,0,2,3:T(2,128)} %copy.2475), calls=%async_computation.2 | async-start | bytes 1048576 | tf_op jit(solution)/shard_map/all_to_all | solution.py:252
  444.2 25.7 %copy-start.229 = (f32[7,2,1]{0,1,2:T(2,128)S(1)}, f32[7,2,1]{0,1,2:T(2,128)}, u32[]{:S(2)}) copy-start(f32[7,2,1]{0,1,2:T(2,128)} %slice.3204) | copy-start | bytes 172
  444.2 26.3 %copy-start.227 = (f32[15,2,1]{0,1,2:T(2,128)S(1)}, f32[15,2,1]{0,1,2:T(2,128)}, u32[]{:S(2)}) copy-start(f32[15,2,1]{0,1,2:T(2,128)} %slice.3197) | copy-start | bytes 364
  444.2 26.5 %copy-start.225 = (f32[31,2,1]{0,1,2:T(2,128)S(1)}, f32[31,2,1]{0,1,2:T(2,128)}, u32[]{:S(2)}) copy-start(f32[31,2,1]{0,1,2:T(2,128)} %slice.3190) | copy-start | bytes 748
  444.2 27.3 %copy-start.223 = (f32[63,2,1]{0,1,2:T(2,128)S(1)}, f32[63,2,1]{0,1,2:T(2,128)}, u32[]{:S(2)}) copy-start(f32[63,2,1]{0,1,2:T(2,128)} %slice.3183) | copy-start | bytes 1516
  444.2 27.8 %copy-start.221 = (f32[127,2,1]{0,1,2:T(2,128)S(1)}, f32[127,2,1]{0,1,2:T(2,128)}, u32[]{:S(2)}) copy-start(f32[127,2,1]{0,1,2:T(2,128)} %slice.3172) | copy-start | bytes 3052
  444.2 29.1 %copy-start.186 = (f32[256,2]{0,1:T(2,128)S(1)}, f32[256,2]{0,1:T(2,128)}, u32[]{:S(2)}) copy-start(f32[256,2]{0,1:T(2,128)} %get-tuple-element.248) | copy-start | bytes 6148
  444.2 29.1 %copy-start.255 = (pred[256]{0:T(512)(128)(4,1)S(1)}, pred[256]{0:T(512)(128)(4,1)}, u32[]{:S(2)}) copy-start(pred[256]{0:T(512)(128)(4,1)} %select_compare_fusion.4) | copy-start | bytes 772
  444.2 29.1 %copy-start.252 = (pred[256]{0:T(512)(128)(4,1)S(1)}, pred[256]{0:T(512)(128)(4,1)}, u32[]{:S(2)}) copy-start(pred[256]{0:T(512)(128)(4,1)} %get-tuple-element.244) | copy-start | bytes 772
  477.1 23.2 %all-to-all-start.3 = ((f32[256,2,2,1,8]{4,2,1,3,0:T(2,128)}), f32[256,2,2,1,8]{4,2,1,3,0:T(2,128)S(1)}, u32[]{:S(2)}, u32[]{:S(2)}) async-start(f32[256,2,2,1,8]{4,2,1,3,0:T(2,128)} %select_bitcast_fusion.2), calls=%async_computation.3 | async-start | bytes 1048576 | tf_op jit(solution)/shard_map/all_to_all | solution.py:254
  511.0 18.4 %all-to-all-start.4 = ((f32[2,2,2,128,8]{4,1,0,2,3:T(2,128)}), f32[2,2,2,128,8]{4,1,0,2,3:T(2,128)S(1)}, u32[]{:S(2)}, u32[]{:S(2)}) async-start(f32[2,2,2,128,8]{4,1,0,2,3:T(2,128)} %copy.2495), calls=%async_computation.4 | async-start | bytes 1048576 | tf_op jit(solution)/shard_map/all_to_all | solution.py:252
  556.6 23.1 %all-to-all-start.5 = ((f32[256,2,2,1,8]{4,1,2,3,0:T(2,128)}), f32[256,2,2,1,8]{4,1,2,3,0:T(2,128)S(1)}, u32[]{:S(2)}, u32[]{:S(2)}) async-start(f32[256,2,2,1,8]{4,1,2,3,0:T(2,128)} %copy.2505), calls=%async_computation.5 | async-start | bytes 1048576 | tf_op jit(solution)/shard_map/all_to_all | solution.py:254
  595.3 18.5 %all-to-all-start.6 = ((f32[2,2,2,128,8]{4,1,0,2,3:T(2,128)}), f32[2,2,2,128,8]{4,1,0,2,3:T(2,128)S(1)}, u32[]{:S(2)}, u32[]{:S(2)}) async-start(f32[2,2,2,128,8]{4,1,0,2,3:T(2,128)} %copy.2514), calls=%async_computation.6 | async-start | bytes 1048576 | tf_op jit(solution)/shard_map/all_to_all | solution.py:252
  (241 other events, 2638.2 us)
where the time goes:
time: 668 us; the launch traced here: 659 us
  local copies, waits for them, and re-layouts  330 us (49%)
  other arithmetic  115 us (17%)
  blocking collectives  89.7 us (13%)
  starting transfers between devices  51.4 us (8%)
  waiting for transfers between devices  48.3 us (7%)
  matrix products  16.1 us (2%)
  between operations  7.91 us (1%)
    unnamed x551, local copies, waits for them, and re-layouts  40.1 us
    all_gather x1, blocking collectives, body(): lax.all_gather(corners, 'bricks', axis=0, tiled=True)  38.2 us
    gather x18, local copies, waits for them, and re-layouts, chain_order(): pointer = jnp.take(pointer, pointer, axis=0)  35 us
    all_gather x1, blocking collectives, body(): lax.all_gather(rates, 'bricks', axis=0, tiled=True)  33.5 us
    slice x147, local copies, waits for them, and re-layouts, sorted_solve(): lax.associative_scan(compose_affine, (-f0[:, :, None], e0), reverse=True,...  31.8 us
    slice x246, local copies, waits for them, and re-layouts, sorted_solve(): summed = lax.associative_scan(compose_maps, maps, axis=0)  31.3 us
    slice x129, local copies, waits for them, and re-layouts, sorted_solve(): e1 = lax.associative_scan(compose_affine, (slope, offset), axis=0)[1]  26.4 us
    all_to_all x2, waiting for transfers between devices, solve(): lax.all_to_all(lined_jumps, 'bricks', split_axis=0, concat_axis=3, tiled=...  25.6 us
  transfers between devices with their start and end apart: 7, of which 6 were waited for; matrix products, arithmetic and copies ran while one was open for 36% of the time, Pallas kernels for 0%

commit v1 on v0

--- a/solution.py
+++ b/solution.py
@@ -210,7 +210,9 @@
         -1,
     )
     rate_all, corner_all = (
-        lax.all_gather(rates, "bricks", axis=0, tiled=True),
+        jnp.concatenate(
+            lax.all_to_all(jnp.stack([rates] * lax.axis_size("bricks")), "bricks", 0, 0), axis=0
+        ),
         lax.all_gather(corners, "bricks", axis=0, tiled=True),
     )
     couple_all = coupling(rate_all, neighbors)

time: 668 us -> 637 us (0.954)
  blocking collectives: 89.7 us -> 56.2 us
  local copies, waits for them, and re-layouts: 330 us -> 321 us
  starting transfers between devices: 51.4 us -> 58.5 us
    all_gather x1 -> x0, blocking collectives: 33.5 us -> none  [body(): lax.all_gather(rates, 'bricks', axis=0, tiled=True)]
    all_to_all x0 -> x1, starting transfers between devices: none -> 11.5 us  [body(): lax.all_to_all(jnp.stack([rates] * lax.axis_size('bricks')), 'bricks', 0, 0)]
    unnamed x551 -> x510, local copies, waits for them, and re-layouts: 40.1 us -> 29.8 us
  transfers between devices with their start and end apart: 7 -> 8, of which waited for: 6 -> 6; matrix products, arithmetic and copies ran while one was open for 36% -> 42% of each run, Pallas kernels for 0% -> 0%
where the time goes in v1:
time: 637 us; the launch traced here: 626 us
  local copies, waits for them, and re-layouts  321 us (50%)
  other arithmetic  117 us (18%)
  starting transfers between devices  58.5 us (9%)
  blocking collectives  56.2 us (9%)
  waiting for transfers between devices  50.5 us (8%)
  matrix products  16.1 us (3%)
  between operations  7.5 us (1%)
    all_gather x1, blocking collectives, body(): lax.all_gather(corners, 'bricks', axis=0, tiled=True)  38.2 us
    gather x18, local copies, waits for them, and re-layouts, chain_order(): pointer = jnp.take(pointer, pointer, axis=0)  35.4 us
    slice x246, local copies, waits for them, and re-layouts, sorted_solve(): summed = lax.associative_scan(compose_maps, maps, axis=0)  31.9 us
    slice x147, local copies, waits for them, and re-layouts, sorted_solve(): lax.associative_scan(compose_affine, (-f0[:, :, None], e0), reverse=True,...  30.7 us
    unnamed x510, local copies, waits for them, and re-layouts  29.8 us
    slice x129, local copies, waits for them, and re-layouts, sorted_solve(): e1 = lax.associative_scan(compose_affine, (slope, offset), axis=0)[1]  26 us
    all_to_all x2, waiting for transfers between devices, solve(): lax.all_to_all(lined_jumps, 'bricks', split_axis=0, concat_axis=3, tiled=...  25.7 us
    all_to_all x1, blocking collectives, solve(): lax.all_to_all(lined_jumps, 'bricks', split_axis=0, concat_axis=3, tiled=...  18 us
  transfers between devices with their start and end apart: 8, of which 6 were waited for; matrix products, arithmetic and copies ran while one was open for 42% of the time, Pallas kernels for 0%

profile of v1, /device:TPU:1, one launch (start us, length us, event | category | flops | bytes accessed | tf_op | source)
XLA Modules:
  0.0 626.5 jit_solution(14922459926014036131)
XLA Ops:
  2.2 11.5 %all-to-all-start = ((f32[128,2,3,2]{2,3,1,0:T(2,128)}), f32[128,2,3,2]{2,3,1,0:T(2,128)S(1)}, u32[]{:S(2)}, u32[]{:S(2)}) async-start(f32[128,2,3,2]{2,3,1,0:T(2,128)} %stack.123), calls=%async_computation | async-start | bytes 524288 | tf_op jit(solution)/shard_map/all_to_all | solution.py:214
  20.9 4.9 divide_add_fusion
  52.0 3.2 sort.87
  55.2 3.2 sort.88
  77.0 3.2 sort.89
  80.1 3.2 sort.90
  101.4 3.2 sort.91
  104.6 3.2 sort.92
  114.4 38.2 %all_gather.3 = f32[256,3,2,4]{1,2,0,3:T(2,128)S(1)} all-gather(f32[2,3,2,4]{1,2,0,3:T(2,128)S(1)} %pad_maximum_fusion.7), channel_id=1, replica_groups=mesh['bricks'=128] {'bricks'}, dimensions={0}, use_global_device_ids=true | all-gather | bytes 24768 | tf_op jit(solution)/shard_map/all_gather | solution.py:216
  152.7 3.6 fusion.208
  187.7 4.2 reshape.1055
  191.9 6.5 %all-to-all-start.1 = ((f32[128,1,192]{2,1,0:T(1,128)}), f32[128,1,192]{2,1,0:T(1,128)}, u32[]{:S(2)}, u32[]{:S(2)}) async-start(f32[128,1,192]{2,1,0:T(1,128)} %reshape.1055), calls=%async_computation.1 | async-start | bytes 262144 | tf_op jit(solution)/shard_map/all_to_all | solution.py:223
  307.4 3.2 reshape.1056
  343.6 4.2 reshape.1057
  347.8 10.3 %all-to-all-start.2 = ((f32[128,1,192]{2,1,0:T(1,128)}), f32[128,1,192]{2,1,0:T(1,128)S(1)}, u32[]{:S(2)}, u32[]{:S(2)}) async-start(f32[128,1,192]{2,1,0:T(1,128)} %reshape.1057), calls=%async_computation.2 | async-start | bytes 262144 | tf_op jit(solution)/shard_map/all_to_all | solution.py:227
  358.9 9.1 %all-to-all-done.2 = f32[128,1,192]{2,1,0:T(1,128)S(1)} async-done(((f32[128,1,192]{2,1,0:T(1,128)}), f32[128,1,192]{2,1,0:T(1,128)S(1)}, u32[]{:S(2)}, u32[]{:S(2)}) %all-to-all-start.2) | async-done | bytes 98336 | tf_op jit(solution)/shard_map/all_to_all | solution.py:227
  383.9 5.0 fusion.18
  391.0 3.8 fusion.31
  397.8 4.3 all-to-all-start.3
  449.8 9.5 %all-to-all-start.4 = ((f32[256,2,2,1,8]{4,2,1,3,0:T(2,128)}), f32[256,2,2,1,8]{4,2,1,3,0:T(2,128)S(1)}, u32[]{:S(2)}, u32[]{:S(2)}) async-start(f32[256,2,2,1,8]{4,2,1,3,0:T(2,128)} %select_bitcast_fusion.2), calls=%async_computation.4 | async-start | bytes 1048576 | tf_op jit(solution)/shard_map/all_to_all | solution.py:256
  460.2 12.6 %all-to-all-done.4 = f32[256,2,2,1,8]{4,2,1,3,0:T(2,128)S(1)} async-done(((f32[256,2,2,1,8]{4,2,1,3,0:T(2,128)}), f32[256,2,2,1,8]{4,2,1,3,0:T(2,128)S(1)}, u32[]{:S(2)}, u32[]{:S(2)}) %all-to-all-start.4) | async-done | bytes 32800 | tf_op jit(solution)/shard_map/all_to_all | solution.py:256
  473.7 3.7 subtract_subtract_fusion.1
  477.4 3.2 fusion.25
  483.4 5.1 all-to-all-start.5
  498.5 3.5 all-to-all-done.5
  527.5 6.6 %all-to-all-start.6 = ((f32[256,2,2,1,8]{4,1,2,3,0:T(2,128)}), f32[256,2,2,1,8]{4,1,2,3,0:T(2,128)S(1)}, u32[]{:S(2)}, u32[]{:S(2)}) async-start(f32[256,2,2,1,8]{4,1,2,3,0:T(2,128)} %copy.2489), calls=%async_computation.6 | async-start | bytes 1048576 | tf_op jit(solution)/shard_map/all_to_all | solution.py:256
  534.5 13.1 %all-to-all-done.6 = f32[256,2,2,1,8]{4,1,2,3,0:T(2,128)S(1)} async-done(((f32[256,2,2,1,8]{4,1,2,3,0:T(2,128)}), f32[256,2,2,1,8]{4,1,2,3,0:T(2,128)S(1)}, u32[]{:S(2)}, u32[]{:S(2)}) %all-to-all-start.6) | async-done | bytes 32800 | tf_op jit(solution)/shard_map/all_to_all | solution.py:256
  548.4 3.7 subtract_subtract_fusion
  552.1 9.1 %fusion.23 = f32[2,2,32,32,32]{3,4,2,1,0:T(8,128)S(1)} fusion(f32[2,2,32,32,32]{4,2,3,1,0:T(8,128)S(1)} %subtract_subtract_fusion, f32[2,3,2,32,32]{4,3,2,1,0:T(8,128)S(1)} %copy-done.14), kind=kOutput, calls=%fused_computation.78 | convolution fusion | flops 50331648 | bytes 2686976 | tf_op jit(solution)/shard_map/psab,psijb->psija/dot_general | solution.py:77
  563.2 4.9 all-to-all-start.7
  570.0 11.5 %all-to-all-done.7 = f32[2,2,2,128,8]{4,1,0,2,3:T(2,128)S(1)} async-done(((f32[2,2,2,128,8]{4,1,0,2,3:T(2,128)}), f32[2,2,2,128,8]{4,1,0,2,3:T(2,128)S(1)}, u32[]{:S(2)}, u32[]{:S(2)}) %all-to-all-start.7) | async-done | bytes 32800 | tf_op jit(solution)/shard_map/all_to_all | solution.py:254
  601.6 18.0 %all_to_all.128 = f32[256,2,2,1,8]{4,1,2,3,0:T(2,128)S(1)} all-to-all(f32[256,2,2,1,8]{4,1,2,3,0:T(2,128)S(1)} %copy.2508), channel_id=1, replica_groups=mesh['bricks'=128] {'bricks'}, dimensions={0} | all-to-all | bytes 65536 | tf_op jit(solution)/shard_map/all_to_all | solution.py:256
  (2075 shorter events, 386.8 us)
Async XLA Ops:
  2.2 189.8 %all-to-all-start = ((f32[128,2,3,2]{2,3,1,0:T(2,128)}), f32[128,2,3,2]{2,3,1,0:T(2,128)S(1)}, u32[]{:S(2)}, u32[]{:S(2)}) async-start(f32[128,2,3,2]{2,3,1,0:T(2,128)} %stack.123), calls=%async_computation | async-start | bytes 524288 | tf_op jit(solution)/shard_map/all_to_all | solution.py:214
  58.3 112.4 %copy-start.33 = (s32[1024]{0:T(1024)}, s32[1024]{0:T(1024)S(1)}, u32[]{:S(2)}) copy-start(s32[1024]{0:T(1024)S(1)} %pad_clamp_fusion.17) | copy-start | bytes 12292
  83.9 82.0 %copy-start.32 = (s32[1024]{0:T(1024)}, s32[1024]{0:T(1024)S(1)}, u32[]{:S(2)}) copy-start(s32[1024]{0:T(1024)S(1)} %pad_clamp_fusion.9) | copy-start | bytes 12292
  108.9 49.7 %copy-start.31 = (s32[1024]{0:T(1024)}, s32[1024]{0:T(1024)S(1)}, u32[]{:S(2)}) copy-start(s32[1024]{0:T(1024)S(1)} %pad_clamp_fusion.1) | copy-start | bytes 12292
  114.0 68.4 %copy-start.35 = (pred[256]{0:T(512)(128)(4,1)}, pred[256]{0:T(512)(128)(4,1)S(1)}, u32[]{:S(2)}) copy-start(pred[256]{0:T(512)(128)(4,1)S(1)} %get-tuple-element.41) | copy-start | bytes 772
  162.4 38.6 %copy-start.170 = (s32[1024]{0:T(1024)}, s32[1024]{0:T(1024)S(1)}, u32[]{:S(2)}) copy-start(s32[1024]{0:T(1024)S(1)} %pad_clamp_fusion.26) | copy-start | bytes 12292
  191.9 113.0 %all-to-all-start.1 = ((f32[128,1,192]{2,1,0:T(1,128)}), f32[128,1,192]{2,1,0:T(1,128)}, u32[]{:S(2)}, u32[]{:S(2)}) async-start(f32[128,1,192]{2,1,0:T(1,128)} %reshape.1055), calls=%async_computation.1 | async-start | bytes 262144 | tf_op jit(solution)/shard_map/all_to_all | solution.py:223
  207.6 25.7 %copy-start.26 = (f32[256,2]{0,1:T(2,128)}, f32[256,2]{0,1:T(2,128)S(1)}, u32[]{:S(2)}) copy-start(f32[256,2]{0,1:T(2,128)S(1)} %get-tuple-element.403) | copy-start | bytes 6148
  267.2 32.5 %copy-start.168 = (f32[4,2,1]{0,1,2:T(2,128)S(1)}, f32[4,2,1]{0,1,2:T(2,128)}, u32[]{:S(2)}) copy-start(f32[4,2,1]{0,1,2:T(2,128)} %copy-done.167) | copy-start | bytes 100
  267.2 33.2 %copy-start.166 = (f32[4,2,1]{0,1,2:T(2,128)S(1)}, f32[4,2,1]{0,1,2:T(2,128)}, u32[]{:S(2)}) copy-start(f32[4,2,1]{0,1,2:T(2,128)} %copy-done.165) | copy-start | bytes 100
  267.2 33.9 %copy-start.101 = (f32[2,2,1]{0,1,2:T(2,128)S(1)}, f32[2,2,1]{0,1,2:T(2,128)}, u32[]{:S(2)}) copy-start(f32[2,2,1]{0,1,2:T(2,128)} %slice.3804) | copy-start | bytes 52
  267.2 33.9 %copy-start.206 = (f32[2,2,1]{0,1,2:T(2,128)S(1)}, f32[2,2,1]{0,1,2:T(2,128)}, u32[]{:S(2)}) copy-start(f32[2,2,1]{0,1,2:T(2,128)} %slice.3808) | copy-start | bytes 52
  268.0 35.7 %copy-start.115 = (f32[2,2,1]{0,1,2:T(2,128)S(1)}, f32[2,2,1]{0,1,2:T(2,128)}, u32[]{:S(2)}) copy-start(f32[2,2,1]{0,1,2:T(2,128)} %slice.3512) | copy-start | bytes 52
  268.0 35.7 %copy-start.207 = (f32[2,2,1]{0,1,2:T(2,128)S(1)}, f32[2,2,1]{0,1,2:T(2,128)}, u32[]{:S(2)}) copy-start(f32[2,2,1]{0,1,2:T(2,128)} %slice.3516) | copy-start | bytes 52
  302.1 81.7 %copy-start.91 = (f32[2,1,1,2]{3,0,2,1:T(2,128)}, f32[2,1,1,2]{3,0,2,1:T(2,128)S(1)}, u32[]{:S(2)}) copy-start(f32[2,1,1,2]{3,0,2,1:T(2,128)S(1)} %copy.2441) | copy-start | bytes 52
  302.2 81.6 %copy-start.93 = (f32[2,1,1,2]{3,0,2,1:T(2,128)}, f32[2,1,1,2]{3,0,2,1:T(2,128)S(1)}, u32[]{:S(2)}) copy-start(f32[2,1,1,2]{3,0,2,1:T(2,128)S(1)} %copy.2443) | copy-start | bytes 52
  302.3 86.7 %copy-start.95 = (f32[2,1,1,2]{3,0,2,1:T(2,128)}, f32[2,1,1,2]{3,0,2,1:T(2,128)S(1)}, u32[]{:S(2)}) copy-start(f32[2,1,1,2]{3,0,2,1:T(2,128)S(1)} %copy.2439) | copy-start | bytes 52
  302.4 86.6 %copy-start.98 = (f32[2,1,1,2]{3,0,2,1:T(2,128)}, f32[2,1,1,2]{3,0,2,1:T(2,128)S(1)}, u32[]{:S(2)}) copy-start(f32[2,1,1,2]{3,0,2,1:T(2,128)S(1)} %copy.2440) | copy-start | bytes 52
  347.8 20.2 %all-to-all-start.2 = ((f32[128,1,192]{2,1,0:T(1,128)}), f32[128,1,192]{2,1,0:T(1,128)S(1)}, u32[]{:S(2)}, u32[]{:S(2)}) async-start(f32[128,1,192]{2,1,0:T(1,128)} %reshape.1057), calls=%async_computation.2 | async-start | bytes 262144 | tf_op jit(solution)/shard_map/all_to_all | solution.py:227
  397.8 17.9 %all-to-all-start.3 = ((f32[2,2,2,128,8]{4,1,0,2,3:T(2,128)}), f32[2,2,2,128,8]{4,1,0,2,3:T(2,128)S(1)}, u32[]{:S(2)}, u32[]{:S(2)}) async-start(f32[2,2,2,128,8]{4,1,0,2,3:T(2,128)} %copy.2459), calls=%async_computation.3 | async-start | bytes 1048576 | tf_op jit(solution)/shard_map/all_to_all | solution.py:254
  416.4 25.9 %copy-start.142 = (f32[2,2,1]{0,1,2:T(2,128)S(1)}, f32[2,2,1]{0,1,2:T(2,128)}, u32[]{:S(2)}) copy-start(f32[2,2,1]{0,1,2:T(2,128)} %copy-done.141) | copy-start | bytes 52
  417.7 26.2 %copy-start.213 = (f32[15,2,1]{0,1,2:T(2,128)S(1)}, f32[15,2,1]{0,1,2:T(2,128)}, u32[]{:S(2)}) copy-start(f32[15,2,1]{0,1,2:T(2,128)} %slice.3197) | copy-start | bytes 364
  417.7 26.4 %copy-start.211 = (f32[31,2,1]{0,1,2:T(2,128)S(1)}, f32[31,2,1]{0,1,2:T(2,128)}, u32[]{:S(2)}) copy-start(f32[31,2,1]{0,1,2:T(2,128)} %slice.3190) | copy-start | bytes 748
  417.7 27.2 %copy-start.210 = (f32[63,2,1]{0,1,2:T(2,128)S(1)}, f32[63,2,1]{0,1,2:T(2,128)}, u32[]{:S(2)}) copy-start(f32[63,2,1]{0,1,2:T(2,128)} %slice.3183) | copy-start | bytes 1516
  417.7 27.7 %copy-start.209 = (f32[127,2,1]{0,1,2:T(2,128)S(1)}, f32[127,2,1]{0,1,2:T(2,128)}, u32[]{:S(2)}) copy-start(f32[127,2,1]{0,1,2:T(2,128)} %slice.3172) | copy-start | bytes 3052
  417.7 29.0 %copy-start.183 = (f32[256,2]{0,1:T(2,128)S(1)}, f32[256,2]{0,1:T(2,128)}, u32[]{:S(2)}) copy-start(f32[256,2]{0,1:T(2,128)} %get-tuple-element.248) | copy-start | bytes 6148
  417.8 29.0 %copy-start.237 = (pred[256]{0:T(512)(128)(4,1)S(1)}, pred[256]{0:T(512)(128)(4,1)}, u32[]{:S(2)}) copy-start(pred[256]{0:T(512)(128)(4,1)} %select_compare_fusion.4) | copy-start | bytes 772
  417.8 29.0 %copy-start.236 = (pred[256]{0:T(512)(128)(4,1)S(1)}, pred[256]{0:T(512)(128)(4,1)}, u32[]{:S(2)}) copy-start(pred[256]{0:T(512)(128)(4,1)} %get-tuple-element.244) | copy-start | bytes 772
  449.8 23.0 %all-to-all-start.4 = ((f32[256,2,2,1,8]{4,2,1,3,0:T(2,128)}), f32[256,2,2,1,8]{4,2,1,3,0:T(2,128)S(1)}, u32[]{:S(2)}, u32[]{:S(2)}) async-start(f32[256,2,2,1,8]{4,2,1,3,0:T(2,128)} %select_bitcast_fusion.2), calls=%async_computation.4 | async-start | bytes 1048576 | tf_op jit(solution)/shard_map/all_to_all | solution.py:256
  483.4 18.6 %all-to-all-start.5 = ((f32[2,2,2,128,8]{4,1,0,2,3:T(2,128)}), f32[2,2,2,128,8]{4,1,0,2,3:T(2,128)S(1)}, u32[]{:S(2)}, u32[]{:S(2)}) async-start(f32[2,2,2,128,8]{4,1,0,2,3:T(2,128)} %copy.2479), calls=%async_computation.5 | async-start | bytes 1048576 | tf_op jit(solution)/shard_map/all_to_all | solution.py:254
  527.5 20.1 %all-to-all-start.6 = ((f32[256,2,2,1,8]{4,1,2,3,0:T(2,128)}), f32[256,2,2,1,8]{4,1,2,3,0:T(2,128)S(1)}, u32[]{:S(2)}, u32[]{:S(2)}) async-start(f32[256,2,2,1,8]{4,1,2,3,0:T(2,128)} %copy.2489), calls=%async_computation.6 | async-start | bytes 1048576 | tf_op jit(solution)/shard_map/all_to_all | solution.py:256
  563.2 18.4 %all-to-all-start.7 = ((f32[2,2,2,128,8]{4,1,0,2,3:T(2,128)}), f32[2,2,2,128,8]{4,1,0,2,3:T(2,128)S(1)}, u32[]{:S(2)}, u32[]{:S(2)}) async-start(f32[2,2,2,128,8]{4,1,0,2,3:T(2,128)} %copy.2498), calls=%async_computation.7 | async-start | bytes 1048576 | tf_op jit(solution)/shard_map/all_to_all | solution.py:254
  (223 other events, 2335.1 us)
